TPU v7x, 256 devices: a whole 4x4x8 slice. The times are simulated.
256 devices in a mesh: pair: 32 (over z, x), occ: 8 (over y, core).
Axes of the slice: x: 4, y: 4, z: 8, core: 2. Of those that a mesh axis runs over, the one named last changes fastest.
Arguments:
- integrals: bfloat16 [32, 256, 64, 1024], P('pair', None, None, 'occ'), may hold values from -6 to 6
- occ_coeffs: bfloat16 [6144, 128], replicated, may hold values from -0.125 to 0.125
- virt_coeffs: bfloat16 [6144, 5120], P(None, 'pair'), may hold values from -0.078125 to 0.078125
- block_ids: int32 [2, 32, 256], P(None, 'pair'), may hold values from 0 to 95, as said below
- live_mask: int32 [32, 256], P('pair'), may hold values from 0 to 1, as said below
Outputs:
- factors: bfloat16 [128, 16, 5120], P('occ', None, 'pair')
Inputs may be any that keep to these rules, and one draw needn't show every extreme that they name: `block_ids`: slot s of pair index p holds a nu block N with N // 3 == s // 8; each (mu block, nu block) pair is held by at most one slot of all pair indices. `live_mask`: among the 8 slots s with the same s // 8 of one pair index, at most 4 are 1, and exactly 4 for some such group of every pair index.
All inputs are finite; a program needn't handle non-finite values.
Results may differ from a plain program's by a relative error of at most 0.017.
Values may be sent and summed in bfloat16 or wider, within the bound.
A program may use at most 64 MiB of HBM per device.

v0:
```python
import jax
import jax.numpy as jnp
from jax import lax
from jax.sharding import PartitionSpec as P

LIVE = 4


def in_one_piece(arrays, axis, split_dim, concat_dim, along):
    both = jnp.concatenate(arrays, axis=along)
    filled, at, done = (
        lax.all_to_all(both, axis, split_axis=split_dim, concat_axis=concat_dim, tiled=True),
        0,
        [],
    )
    for a in arrays:
        done.append(lax.slice_in_dim(filled, at, at + a.shape[along], axis=along))
        at += a.shape[along]
    return tuple(done)


def half_transform(block_data, mu_index, coeff_blocks):
    slot_count, block_width = (block_data.shape[0], block_data.shape[1])
    aux_local = block_data.shape[2] // block_width
    coeff_rows = jnp.take(coeff_blocks, mu_index, axis=0)
    shaped = block_data.reshape(slot_count, block_width, aux_local, block_width)
    return jnp.einsum("snqm,smi->snqi", shaped, coeff_rows, preferred_element_type=jnp.float32)


def on_device(integrals, occ_coeffs, virt_coeffs, block_ids, live_mask):
    blocks = integrals[0]
    slot_count, block_width = (blocks.shape[0], blocks.shape[1])
    aux_local = blocks.shape[2] // block_width
    occ_count = occ_coeffs.shape[1]
    block_count = occ_coeffs.shape[0] // block_width
    owners = lax.axis_size("pair")
    owned_count = block_count // owners
    group_size = slot_count // owners
    coeff_blocks = occ_coeffs.reshape(block_count, block_width, occ_count)
    mu_index = block_ids[0, 0]
    nu_index = block_ids[1, 0]
    live_flags = live_mask[0]
    grouped_live = live_flags.reshape(owners, group_size)
    sort_keys = (1 - grouped_live) * group_size + jnp.arange(group_size)[None, :]
    chosen = jnp.argsort(sort_keys, axis=1)[:, :LIVE]
    valid_flags = jnp.take_along_axis(grouped_live, chosen, axis=1).reshape(-1)
    slot_index = (chosen + jnp.arange(owners)[:, None] * group_size).reshape(-1)
    send_blocks = blocks[slot_index] * valid_flags[:, None, None].astype(jnp.bfloat16)
    send_blocks = send_blocks.reshape(owners, LIVE, block_width, aux_local * block_width)
    send_mu = mu_index[slot_index].reshape(owners, LIVE)
    send_nu = nu_index[slot_index].reshape(owners, LIVE)
    got_blocks, got_mu, got_nu = (
        lax.all_to_all(send_blocks, "pair", split_axis=0, concat_axis=0, tiled=True),
        *in_one_piece((send_mu, send_nu), "pair", 0, 0, 1),
    )
    partial_terms = half_transform(
        got_blocks.reshape(owners * LIVE, block_width, -1), got_mu.reshape(-1), coeff_blocks
    )
    selector = got_nu.reshape(-1)[None, :] % owned_count == jnp.arange(owned_count)[:, None]
    summed = jnp.dot(
        selector.astype(jnp.float32),
        partial_terms.reshape(owners * LIVE, -1),
        precision=lax.Precision.HIGHEST,
    )
    summed = summed.reshape(owned_count, block_width, aux_local, occ_count)
    half_sums = summed.astype(jnp.bfloat16)
    slab_sums = lax.all_to_all(half_sums, "occ", split_axis=3, concat_axis=2, tiled=True)
    aux_count, slab_rows = (slab_sums.shape[2], slab_sums.shape[3])
    shard_piece = lax.all_gather(slab_sums, "pair", axis=0, tiled=True)
    piece_blocks = shard_piece.shape[0]
    flat_piece = shard_piece.reshape(piece_blocks * block_width, aux_count, slab_rows)
    result = jnp.einsum("nqi,na->iqa", flat_piece, virt_coeffs, preferred_element_type=jnp.float32)
    return result.astype(jnp.bfloat16)


def solution(mesh):
    return jax.shard_map(
        on_device,
        mesh=mesh,
        in_specs=(
            P("pair", None, None, "occ"),
            P(),
            P(None, "pair"),
            P(None, "pair", None),
            P("pair", None),
        ),
        out_specs=P("occ", None, "pair"),
        check_vma=False,
    )
```

profile of v0, /device:TPU:1, one launch (start us, length us, event | category | flops | bytes accessed | tf_op | source)
XLA Modules:
  0.0 251.1 jit_solution(16702428918213110654)
XLA Ops:
  6.5 0.0 copy-start
  6.5 0.8 fusion.25
  7.4 0.5 broadcast.123
  7.9 1.3 reduce.3
  9.2 0.1 reshape_squeeze.3
  9.3 0.1 copy.50
  9.4 0.7 sort.17
  10.1 0.1 copy.53
  10.2 0.1 reshape.179
  10.3 1.3 gather_fusion.4
  11.6 0.1 reshape.182
  11.7 0.1 copy.54
  11.7 0.1 copy.51
  11.8 0.1 reshape.138
  12.0 1.3 gather_fusion.1
  13.2 1.3 gather_fusion
  14.5 0.1 reshape.139
  14.6 0.1 reshape.140
  14.7 0.7 pad_add_fusion
  15.4 11.9 %all-to-all-start = ((s32[32,1,8]{2,1,0:T(1,128)}), s32[32,1,8]{2,1,0:T(1,128)S(1)}, u32[]{:S(2)}, u32[]{:S(2)}) async-start(s32[32,1,8]{2,1,0:T(1,128)} %bitcast.4), calls=%async_computation | async-start | bytes 32768 | tf_op jit(solution)/shard_map/all_to_all | solution.py:12
  27.3 0.1 copy.55
  27.4 4.3 %gather_fusion.2 = bf16[128,64,128]{2,1,0:T(8,128)(2,1)} fusion(bf16[256,64,128]{2,1,0:T(8,128)(2,1)} %bitcast.62, s32[1024]{0:T(1024)S(1)} %pad_clamp_fusion.1), kind=kCustom, calls=%fused_computation.2 | custom fusion | bytes 4194816 | tf_op jit(solution)/shard_map/gather | solution.py:48
  31.7 3.1 %broadcast_multiply_fusion = bf16[32,4,64,128]{3,2,1,0:T(8,128)(2,1)} fusion(bf16[32,4,64,128]{3,2,1,0:T(8,128)(2,1)} %bitcast.60, bf16[32,4]{1,0:T(8,128)(2,1)S(1)} %copy.55), kind=kLoop, calls=%fused_computation.18 | loop fusion | flops 1048576 | bytes 4194560 | tf_op jit(solution)/shard_map/mul | solution.py:48
  34.8 0.0 copy-start.1
  34.8 1.0 all-to-all-done
  35.8 8.5 %all-to-all-start.1 = ((bf16[32,4,64,128]{3,2,1,0:T(8,128)(2,1)}), bf16[32,4,64,128]{3,2,1,0:T(8,128)(2,1)}, u32[]{:S(2)}, u32[]{:S(2)}) async-start(bf16[32,4,64,128]{3,2,1,0:T(8,128)(2,1)} %broadcast_multiply_fusion), calls=%async_computation.1 | async-start | bytes 4194304 | tf_op jit(solution)/shard_map/all_to_all | solution.py:53
  44.3 0.0 all-gather.2.cloned.1.call-start
  44.4 0.7 slice_remainder_fusion
  45.1 0.8 reshape.144
  45.9 0.8 reshape.142
  46.7 0.8 rem.20
  47.6 0.0 copy-done.1
  47.6 2.2 gather_fusion.3
  49.7 42.5 %all-to-all-done.1 = bf16[32,4,64,128]{3,2,1,0:T(8,128)(2,1)} async-done(((bf16[32,4,64,128]{3,2,1,0:T(8,128)(2,1)}), bf16[32,4,64,128]{3,2,1,0:T(8,128)(2,1)}, u32[]{:S(2)}, u32[]{:S(2)}) %all-to-all-start.1) | async-done | bytes 2097184 | tf_op jit(solution)/shard_map/all_to_all | solution.py:53
  92.3 8.2 %reshape_reshape.3 = bf16[128,64,2,64]{3,2,1,0:T(2,128)(2,1)} reshape(bf16[32,4,64,128]{3,2,1,0:T(8,128)(2,1)} %all-to-all-done.1) | data formatting | bytes 4194304 | tf_op jit(solution)/shard_map/reshape;reshape | solution.py:26
  100.5 7.4 %fusion.2 = f32[128,64,2,128]{3,1,2,0:T(8,128)} fusion(bf16[128,64,2,64]{3,2,1,0:T(2,128)(2,1)} %reshape_reshape.3, bf16[128,64,128]{2,1,0:T(8,128)(2,1)} %gather_fusion.3, pred[128]{0:T(512)(128)(4,1)S(1)} %compare_and_fusion), kind=kOutput, calls=%fused_computation.7 | convolution fusion | flops 269484032 | bytes 12583040 | tf_op jit(solution)/shard_map/snqm,smi->snqi/dot_general | solution.py:27
  107.9 9.2 %copy.57 = f32[128,64,2,128]{0,3,2,1:T(8,128)} copy(f32[128,64,2,128]{3,1,2,0:T(8,128)} %fusion.2) | data formatting | bytes 16777216 | tf_op jit(solution)/shard_map/snqm,smi->snqi/dot_general | solution.py:27
  117.1 7.1 %fusion.12 = bf16[3,64,2,128]{3,0,2,1:T(4,128)(2,1)S(1)} fusion(f32[128,64,2,128]{0,3,2,1:T(8,128)} %copy.57, s32[128]{0:T(128)S(1)} %and_select_fusion), kind=kOutput, calls=%fused_computation.15 | convolution fusion | flops 75547008 | bytes 8487424 | tf_op jit(solution)/shard_map/dot_general | solution.py:60
  124.2 0.2 copy.58
  124.4 0.2 reshape.202
  124.6 12.4 %all_to_all.35 = bf16[8,2,3072]{2,1,0:T(2,128)(2,1)S(1)} all-to-all(bf16[8,2,3072]{2,1,0:T(2,128)(2,1)S(1)} %reshape.202), channel_id=1, replica_groups=mesh['pair'=32,'occ'=8] {'occ'}, dimensions={0} | all-to-all | bytes 196608 | tf_op jit(solution)/shard_map/all_to_all | solution.py:67
  137.0 0.2 reshape.203
  137.2 0.7 copy.60
  137.9 0.0 all-gather.2.cloned.1.call-update
  137.9 84.2 %all-gather.2.cloned.1.call-done = bf16[96,64,16,16]{1,3,2,0:T(8,128)(2,1)} async-done(((bf16[3,64,16,16]{1,3,2,0:T(8,128)(2,1)}), bf16[96,64,16,16]{1,3,2,0:T(8,128)(2,1)}) %all-gather.2.cloned.1.call-update) | async-done | bytes 3145744 | tf_op jit(solution)/shard_map/all_gather | solution.py:69
  222.1 9.5 %copy.61 = bf16[96,64,16,16]{1,0,3,2:T(8,128)(2,1)} copy(bf16[96,64,16,16]{1,3,2,0:T(8,128)(2,1)} %all-gather.2.cloned.1.call-done) | data formatting | bytes 6291456 | tf_op jit(solution)/shard_map/all_gather | solution.py:69
  231.6 9.1 %reshape.146 = bf16[6144,16,16]{0,2,1:T(8,128)(2,1)} reshape(bf16[96,64,16,16]{1,0,3,2:T(8,128)(2,1)} %copy.61) | data formatting | bytes 6291456 | tf_op jit(solution)/shard_map/reshape | solution.py:71
  240.7 0.0 copy-done
  240.7 2.9 %fusion.15 = bf16[16,16,160]{2,0,1:T(8,128)(2,1)S(1)} fusion(bf16[6144,16,16]{0,2,1:T(8,128)(2,1)} %reshape.146, bf16[6144,160]{0,1:T(8,128)(2,1)S(1)} %copy-done), kind=kOutput, calls=%fused_computation.16 | convolution fusion | flops 503357440 | bytes 5193728 | tf_op jit(solution)/shard_map/nqi,na->iqa/dot_general | solution.py:72
  243.6 0.7 copy.62
  (12 shorter events, 0.1 us)
Async XLA Ops:
  6.5 234.1 %copy-start = (bf16[6144,160]{0,1:T(8,128)(2,1)S(1)}, bf16[6144,160]{0,1:T(8,128)(2,1)}, u32[]{:S(2)}) copy-start(bf16[6144,160]{0,1:T(8,128)(2,1)} %param.7) | copy-start | bytes 5898244
  15.4 20.4 %all-to-all-start = ((s32[32,1,8]{2,1,0:T(1,128)}), s32[32,1,8]{2,1,0:T(1,128)S(1)}, u32[]{:S(2)}, u32[]{:S(2)}) async-start(s32[32,1,8]{2,1,0:T(1,128)} %bitcast.4), calls=%async_computation | async-start | bytes 32768 | tf_op jit(solution)/shard_map/all_to_all | solution.py:12
  34.8 12.7 %copy-start.1 = (bf16[6144,128]{1,0:T(8,128)(2,1)S(1)}, bf16[6144,128]{1,0:T(8,128)(2,1)}, u32[]{:S(2)}) copy-start(bf16[6144,128]{1,0:T(8,128)(2,1)} %param.6) | copy-start | bytes 4718596
  35.8 56.5 %all-to-all-start.1 = ((bf16[32,4,64,128]{3,2,1,0:T(8,128)(2,1)}), bf16[32,4,64,128]{3,2,1,0:T(8,128)(2,1)}, u32[]{:S(2)}, u32[]{:S(2)}) async-start(bf16[32,4,64,128]{3,2,1,0:T(8,128)(2,1)} %broadcast_multiply_fusion), calls=%async_computation.1 | async-start | bytes 4194304 | tf_op jit(solution)/shard_map/all_to_all | solution.py:53
  44.3 177.8 %all-gather.2.cloned.1.call-start = ((), (), s32[]{:S(2)}) async-start(), calls=%async_computation.3 | async-start | bytes 6488064 | tf_op jit(solution)/shard_map/all_gather | solution.py:69
Sparse Core Ops, SparseCore 0:
  138.0 84.0 all-gather.1
where the time goes:
time: 252 us; the launch traced here: 251 us
  waiting for transfers between devices  128 us (51%)
  local copies, waits for them, and re-layouts  53.1 us (21%)
  starting transfers between devices  20.4 us (8%)
  matrix products  17.4 us (7%)
  between operations  13.6 us (5%)
  blocking collectives  12.4 us (5%)
  other arithmetic  6.55 us (3%)
    all_gather x1, waiting for transfers between devices, on_device(): shard_piece = lax.all_gather(slab_sums, 'pair', axis=0, tiled=True)  84.2 us
    all_to_all x1, waiting for transfers between devices, on_device(): lax.all_to_all(send_blocks, 'pair', split_axis=0, concat_axis=0, tiled=True)  42.5 us
    all_to_all x1, blocking collectives, on_device(): lax.all_to_all(half_sums, 'occ', split_axis=3, concat_axis=2, tiled=True)  12.4 us
    all_to_all x1, starting transfers between devices, in_one_piece(): lax.all_to_all(both, axis, split_axis=split_dim, concat_axis=concat_dim,...  11.9 us
    all_gather x1, local copies, waits for them, and re-layouts, on_device(): shard_piece = lax.all_gather(slab_sums, 'pair', axis=0, tiled=True)  9.49 us
    dot_general x1, local copies, waits for them, and re-layouts, half_transform(): jnp.einsum('snqm,smi->snqi', shaped, coeff_rows, preferred_element_type=j...  9.2 us
    reshape x1, local copies, waits for them, and re-layouts, on_device(): shard_piece.reshape(piece_blocks * block_width, aux_count, slab_rows)  9.09 us
    all_to_all x1, starting transfers between devices, on_device(): lax.all_to_all(send_blocks, 'pair', split_axis=0, concat_axis=0, tiled=True)  8.52 us
  transfers between devices with their start and end apart: 3, of which 3 were waited for; matrix products, arithmetic and copies ran while one was open for 5% of the time, Pallas kernels for 0%

commit v1 on v0

--- a/solution.py
+++ b/solution.py
@@ -66,7 +66,8 @@
     half_sums = summed.astype(jnp.bfloat16)
     slab_sums = lax.all_to_all(half_sums, "occ", split_axis=3, concat_axis=2, tiled=True)
     aux_count, slab_rows = (slab_sums.shape[2], slab_sums.shape[3])
-    shard_piece = lax.all_gather(slab_sums, "pair", axis=0, tiled=True)
+    sent = jnp.stack([slab_sums] * lax.axis_size("pair"))
+    shard_piece = jnp.concatenate(lax.all_to_all(sent, "pair", 0, 0), axis=0)
     piece_blocks = shard_piece.shape[0]
     flat_piece = shard_piece.reshape(piece_blocks * block_width, aux_count, slab_rows)
     result = jnp.einsum("nqi,na->iqa", flat_piece, virt_coeffs, preferred_element_type=jnp.float32)

time: 252 us -> 262 us (1.040); the launches traced: 251 us -> 258 us
  waiting for transfers between devices: 128 us -> 43.5 us
  blocking collectives: 12.4 us -> 89.2 us
  local copies, waits for them, and re-layouts: 53.1 us -> 81.1 us
  between operations: 13.6 us -> 0.18 us
    all_gather x1 -> x0, waiting for transfers between devices: 84.2 us -> none  [on_device(): shard_piece = lax.all_gather(slab_sums, 'pair', axis=0, tiled=True)]
    all_to_all x0 -> x1, blocking collectives: none -> 76.7 us  [on_device(): shard_piece = jnp.concatenate(lax.all_to_all(sent, 'pair', 0, 0), axis=0)]
    unnamed x7 -> x10, local copies, waits for them, and re-layouts: 0.86 us -> 22.7 us
    another operation x0 -> x1, local copies, waits for them, and re-layouts: none -> 14.1 us  [on_device(): shard_piece.reshape(piece_blocks * block_width, aux_count, slab_rows)]
    all_to_all x0 -> x1, local copies, waits for them, and re-layouts: none -> 11.4 us  [on_device(): shard_piece = jnp.concatenate(lax.all_to_all(sent, 'pair', 0, 0), axis=0)]
    all_gather x1 -> x0, local copies, waits for them, and re-layouts: 9.49 us -> none  [on_device(): shard_piece = lax.all_gather(slab_sums, 'pair', axis=0, tiled=True)]
    reshape x1 -> x0, local copies, waits for them, and re-layouts: 9.09 us -> none  [on_device(): shard_piece.reshape(piece_blocks * block_width, aux_count, slab_rows)]
  transfers between devices with their start and end apart: 3 -> 2, of which waited for: 3 -> 2; matrix products, arithmetic and copies ran while one was open for 5% -> 5% of each run, Pallas kernels for 0% -> 0%
where the time goes in v1:
time: 262 us; the launch traced here: 258 us
  blocking collectives  89.2 us (34%)
  local copies, waits for them, and re-layouts  81.1 us (31%)
  waiting for transfers between devices  43.5 us (17%)
  starting transfers between devices  20.4 us (8%)
  matrix products  17.4 us (7%)
  other arithmetic  6.54 us (2%)
    all_to_all x1, blocking collectives, on_device(): shard_piece = jnp.concatenate(lax.all_to_all(sent, 'pair', 0, 0), axis=0)  76.7 us
    all_to_all x1, waiting for transfers between devices, on_device(): lax.all_to_all(send_blocks, 'pair', split_axis=0, concat_axis=0, tiled=True)  42.5 us
    unnamed x10, local copies, waits for them, and re-layouts  22.7 us
    another operation x1, local copies, waits for them, and re-layouts, on_device(): shard_piece.reshape(piece_blocks * block_width, aux_count, slab_rows)  14.1 us
    all_to_all x1, blocking collectives, on_device(): lax.all_to_all(half_sums, 'occ', split_axis=3, concat_axis=2, tiled=True)  12.4 us
    all_to_all x1, starting transfers between devices, in_one_piece(): lax.all_to_all(both, axis, split_axis=split_dim, concat_axis=concat_dim,...  11.9 us
    all_to_all x1, local copies, waits for them, and re-layouts, on_device(): shard_piece = jnp.concatenate(lax.all_to_all(sent, 'pair', 0, 0), axis=0)  11.4 us
    dot_general x1, local copies, waits for them, and re-layouts, half_transform(): jnp.einsum('snqm,smi->snqi', shaped, coeff_rows, preferred_element_type=j...  9.17 us
  transfers between devices with their start and end apart: 2, of which 2 were waited for; matrix products, arithmetic and copies ran while one was open for 5% of the time, Pallas kernels for 0%

profile of v1, /device:TPU:1, one launch (start us, length us, event | category | flops | bytes accessed | tf_op | source)
XLA Modules:
  0.0 258.3 jit_solution(2381215507269856049)
XLA Ops:
  0.0 0.0 copy-start
  0.0 0.8 fusion.25
  0.8 0.5 broadcast.124
  1.4 1.3 reduce.3
  2.7 0.1 reshape_squeeze.3
  2.8 0.1 copy.50
  2.9 0.7 sort.17
  3.5 0.1 copy.53
  3.6 0.1 reshape.178
  3.7 1.3 gather_fusion.4
  5.0 0.1 reshape.181
  5.1 0.1 copy.54
  5.2 0.1 copy.51
  5.3 0.1 reshape.138
  5.4 1.3 gather_fusion.1
  6.7 1.3 gather_fusion
  8.0 0.1 reshape.139
  8.1 0.1 reshape.140
  8.2 0.7 pad_add_fusion
  8.9 11.9 %all-to-all-start = ((s32[32,1,8]{2,1,0:T(1,128)}), s32[32,1,8]{2,1,0:T(1,128)S(1)}, u32[]{:S(2)}, u32[]{:S(2)}) async-start(s32[32,1,8]{2,1,0:T(1,128)} %bitcast.4), calls=%async_computation | async-start | bytes 32768 | tf_op jit(solution)/shard_map/all_to_all | solution.py:12
  20.8 0.1 copy.55
  20.9 4.4 %gather_fusion.2 = bf16[128,64,128]{2,1,0:T(8,128)(2,1)} fusion(bf16[256,64,128]{2,1,0:T(8,128)(2,1)} %bitcast.64, s32[1024]{0:T(1024)S(1)} %pad_clamp_fusion.1), kind=kCustom, calls=%fused_computation.2 | custom fusion | bytes 4194816 | tf_op jit(solution)/shard_map/gather | solution.py:48
  25.2 3.1 %broadcast_multiply_fusion = bf16[32,4,64,128]{3,2,1,0:T(8,128)(2,1)} fusion(bf16[32,4,64,128]{3,2,1,0:T(8,128)(2,1)} %bitcast.62, bf16[32,4]{1,0:T(8,128)(2,1)S(1)} %copy.55), kind=kLoop, calls=%fused_computation.18 | loop fusion | flops 1048576 | bytes 4194560 | tf_op jit(solution)/shard_map/mul | solution.py:48
  28.3 0.0 copy-start.1
  28.3 1.0 all-to-all-done
  29.3 8.5 %all-to-all-start.1 = ((bf16[32,4,64,128]{3,2,1,0:T(8,128)(2,1)}), bf16[32,4,64,128]{3,2,1,0:T(8,128)(2,1)}, u32[]{:S(2)}, u32[]{:S(2)}) async-start(bf16[32,4,64,128]{3,2,1,0:T(8,128)(2,1)} %broadcast_multiply_fusion), calls=%async_computation.1 | async-start | bytes 4194304 | tf_op jit(solution)/shard_map/all_to_all | solution.py:53
  37.8 0.7 slice_remainder_fusion
  38.5 0.8 reshape.144
  39.3 0.8 reshape.142
  40.1 0.8 rem.20
  41.0 0.0 copy-done.1
  41.0 2.2 gather_fusion.3
  43.2 42.5 %all-to-all-done.1 = bf16[32,4,64,128]{3,2,1,0:T(8,128)(2,1)} async-done(((bf16[32,4,64,128]{3,2,1,0:T(8,128)(2,1)}), bf16[32,4,64,128]{3,2,1,0:T(8,128)(2,1)}, u32[]{:S(2)}, u32[]{:S(2)}) %all-to-all-start.1) | async-done | bytes 2097184 | tf_op jit(solution)/shard_map/all_to_all | solution.py:53
  85.7 8.2 %reshape_reshape.6 = bf16[128,64,2,64]{3,2,1,0:T(2,128)(2,1)} reshape(bf16[32,4,64,128]{3,2,1,0:T(8,128)(2,1)} %all-to-all-done.1) | data formatting | bytes 4194304 | tf_op jit(solution)/shard_map/reshape;reshape | solution.py:26
  93.9 7.4 %fusion.2 = f32[128,64,2,128]{3,1,2,0:T(8,128)} fusion(bf16[128,64,2,64]{3,2,1,0:T(2,128)(2,1)} %reshape_reshape.6, bf16[128,64,128]{2,1,0:T(8,128)(2,1)} %gather_fusion.3, pred[128]{0:T(512)(128)(4,1)S(1)} %compare_and_fusion), kind=kOutput, calls=%fused_computation.7 | convolution fusion | flops 269484032 | bytes 12583040 | tf_op jit(solution)/shard_map/snqm,smi->snqi/dot_general | solution.py:27
  101.3 9.2 %copy.57 = f32[128,64,2,128]{0,3,2,1:T(8,128)} copy(f32[128,64,2,128]{3,1,2,0:T(8,128)} %fusion.2) | data formatting | bytes 16777216 | tf_op jit(solution)/shard_map/snqm,smi->snqi/dot_general | solution.py:27
  110.5 7.1 %fusion.12 = bf16[3,64,2,128]{3,0,2,1:T(4,128)(2,1)S(1)} fusion(f32[128,64,2,128]{0,3,2,1:T(8,128)} %copy.57, s32[128]{0:T(128)S(1)} %and_select_fusion), kind=kOutput, calls=%fused_computation.15 | convolution fusion | flops 75547008 | bytes 8487424 | tf_op jit(solution)/shard_map/dot_general | solution.py:60
  117.6 0.2 copy.58
  117.8 0.2 reshape.201
  118.0 12.4 %all_to_all.37 = bf16[8,2,3072]{2,1,0:T(2,128)(2,1)S(1)} all-to-all(bf16[8,2,3072]{2,1,0:T(2,128)(2,1)S(1)} %reshape.201), channel_id=1, replica_groups=mesh['pair'=32,'occ'=8] {'occ'}, dimensions={0} | all-to-all | bytes 196608 | tf_op jit(solution)/shard_map/all_to_all | solution.py:67
  130.4 0.2 reshape.202
  130.7 4.2 %broadcast_bitcast_fusion = bf16[32,3,16,16,64]{4,3,2,1,0:T(8,128)(2,1)} fusion(bf16[3,64,16,16]{1,3,2,0:T(8,128)(2,1)S(1)} %bitcast.65), kind=kLoop, calls=%fused_computation.41 | loop fusion | bytes 3244032
  134.9 8.8 %reshape.203 = bf16[32,2,24576]{2,1,0:T(2,128)(2,1)} reshape(bf16[32,3,16,16,64]{4,3,2,1,0:T(8,128)(2,1)} %broadcast_bitcast_fusion) | data formatting | bytes 6291456
  143.7 76.7 %all_to_all.38 = bf16[32,2,24576]{2,1,0:T(2,128)(2,1)} all-to-all(bf16[32,2,24576]{2,1,0:T(2,128)(2,1)} %reshape.203), channel_id=1, replica_groups=mesh['pair'=32,'occ'=8] {'pair'}, dimensions={0} | all-to-all | bytes 6291456 | tf_op jit(solution)/shard_map/all_to_all | solution.py:70
  220.4 8.8 %reshape.204 = bf16[32,3,16,16,64]{4,3,2,1,0:T(8,128)(2,1)} reshape(bf16[32,2,24576]{2,1,0:T(2,128)(2,1)} %all_to_all.38) | data formatting | bytes 6291456
  229.2 11.4 %copy.61 = bf16[32,3,64,16,16]{2,1,0,4,3:T(4,128)(2,1)} copy(bf16[32,3,64,16,16]{2,4,3,1,0:T(8,128)(2,1)} %bitcast.61) | data formatting | bytes 6291456 | tf_op jit(solution)/shard_map/all_to_all | solution.py:70
  240.6 14.1 %reshape_reshape.7 = bf16[6144,16,16]{0,2,1:T(8,128)(2,1)} reshape(bf16[32,3,64,16,16]{2,1,0,4,3:T(4,128)(2,1)} %copy.61) | data formatting | bytes 6291456 | tf_op jit(solution)/shard_map/reshape;reshape | solution.py:72
  254.7 0.0 copy-done
  254.7 2.9 %fusion.15 = bf16[16,16,160]{2,0,1:T(8,128)(2,1)S(1)} fusion(bf16[6144,16,16]{0,2,1:T(8,128)(2,1)} %reshape_reshape.7, bf16[6144,160]{0,1:T(8,128)(2,1)S(1)} %copy-done), kind=kOutput, calls=%fused_computation.16 | convolution fusion | flops 503357440 | bytes 5193728 | tf_op jit(solution)/shard_map/nqi,na->iqa/dot_general | solution.py:73
  257.6 0.7 copy.62
  (13 shorter events, 0.1 us)
Async XLA Ops:
  0.0 254.7 %copy-start = (bf16[6144,160]{0,1:T(8,128)(2,1)S(1)}, bf16[6144,160]{0,1:T(8,128)(2,1)}, u32[]{:S(2)}) copy-start(bf16[6144,160]{0,1:T(8,128)(2,1)} %param.7) | copy-start | bytes 5898244
  8.9 20.4 %all-to-all-start = ((s32[32,1,8]{2,1,0:T(1,128)}), s32[32,1,8]{2,1,0:T(1,128)S(1)}, u32[]{:S(2)}, u32[]{:S(2)}) async-start(s32[32,1,8]{2,1,0:T(1,128)} %bitcast.4), calls=%async_computation | async-start | bytes 32768 | tf_op jit(solution)/shard_map/all_to_all | solution.py:12
  28.3 12.7 %copy-start.1 = (bf16[6144,128]{1,0:T(8,128)(2,1)S(1)}, bf16[6144,128]{1,0:T(8,128)(2,1)}, u32[]{:S(2)}) copy-start(bf16[6144,128]{1,0:T(8,128)(2,1)} %param.6) | copy-start | bytes 4718596
  29.3 56.5 %all-to-all-start.1 = ((bf16[32,4,64,128]{3,2,1,0:T(8,128)(2,1)}), bf16[32,4,64,128]{3,2,1,0:T(8,128)(2,1)}, u32[]{:S(2)}, u32[]{:S(2)}) async-start(bf16[32,4,64,128]{3,2,1,0:T(8,128)(2,1)} %broadcast_multiply_fusion), calls=%async_computation.1 | async-start | bytes 4194304 | tf_op jit(solution)/shard_map/all_to_all | solution.py:53
